TPU v7x, 32 devices: a whole 2x2x4 slice. The times are simulated.
32 devices in a mesh: grp: 2 (over x), row: 8 (over z, y), col: 2 (over core).
Axes of the slice: x: 2, y: 2, z: 4, core: 2. Of those that a mesh axis runs over, the one named last changes fastest.
Arguments:
- queries: bfloat16 [128, 32, 1024], P(('grp', 'row'), 'col'), parts along dimension 0, may hold values from -4 to 4
- key_map: bfloat16 [128, 32, 1024], P(('grp', 'row'), 'col'), parts along dimension 0, may hold values from -4 to 4
- value_map: bfloat16 [128, 32, 1024], P(('grp', 'row'), 'col'), parts along dimension 0, may hold values from -4 to 4
- saved_output: bfloat16 [128, 32, 1024], P(('grp', 'row'), 'col'), parts along dimension 0, may hold values from -4 to 4, as said below
- output_grad: bfloat16 [128, 32, 1024], P(('grp', 'row'), 'col'), parts along dimension 0, may hold values from -48 to 48
- saved_logsum: float32 [128, 32, 16], P(('grp', 'row'), 'col'), parts along dimension 0, may hold values from -128 to 140, as said below
Outputs:
- query_grad: float32 [128, 32, 1024], P(('grp', 'row'), 'col'), parts along dimension 0
- key_grad: float32 [128, 32, 1024], P(('grp', 'row'), 'col'), parts along dimension 0
- value_grad: float32 [128, 32, 1024], P(('grp', 'row'), 'col'), parts along dimension 0
There are 2 independent parts, one for each index of `grp`. A program takes and returns all parts, laid end to end along the dimension named above; each array names one. Nothing has to cross between parts.
Inputs may be any that keep to these rules, and one draw needn't show every extreme that they name: `saved_output`: the attention output of these queries, keys and values over the stripes of the steps, sum over j of softmax of scores times value_map[j], rounded to bfloat16. `saved_logsum`: for each token and head, the natural logarithm of the sum of exp(scores) over the keys of its stripe.
All inputs are finite; a program needn't handle non-finite values.
Results may differ from a plain program's by a relative error of at most 0.003.
Values may be sent and summed in bfloat16 or wider, within the bound.
A program may use at most 128 MiB of HBM per device.

v0:
```python
import math
import jax
import jax.numpy as jnp
from jax import lax
from jax.sharding import PartitionSpec as P

HEADS = 16
HD = 64
SW = 8


def attention_terms(
    stripe_query, stripe_key, stripe_value, stripe_grad, stripe_logsum, stripe_delta
):
    scale = 1.0 / math.sqrt(HD)
    scores = (
        jnp.einsum("gahe,gbhe->ghab", stripe_query, stripe_key, preferred_element_type=jnp.float32)
        * scale
    )
    probs = jnp.exp(scores - jnp.swapaxes(stripe_logsum, 1, 2)[..., None])
    grad_probs = jnp.einsum(
        "gahe,gbhe->ghab", stripe_grad, stripe_value, preferred_element_type=jnp.float32
    )
    grad_scores = (probs * (grad_probs - jnp.swapaxes(stripe_delta, 1, 2)[..., None])).astype(
        jnp.bfloat16
    )
    return (probs.astype(jnp.bfloat16), grad_scores)


def query_side(grad_scores, stripe_key):
    total = jnp.einsum(
        "ghab,gbhe->gahe", grad_scores, stripe_key, preferred_element_type=jnp.float32
    )
    return total * (1.0 / math.sqrt(HD))


def key_side(probs_half, grad_scores, stripe_query, stripe_grad):
    key_total = jnp.einsum(
        "ghab,gahe->gbhe", grad_scores, stripe_query, preferred_element_type=jnp.float32
    )
    value_total = jnp.einsum(
        "ghab,gahe->gbhe", probs_half, stripe_grad, preferred_element_type=jnp.float32
    )
    return (key_total * (1.0 / math.sqrt(HD)), value_total)


def in_blocks(step, carry, arrays, size):
    length = arrays[0].shape[0]

    def turn(index, total):
        parts = tuple((lax.dynamic_slice_in_dim(array, index * size, size, 0) for array in arrays))
        return step(total, parts)

    return lax.fori_loop(0, length // size, turn, carry)


def local(queries, key_map, value_map, saved_output, output_grad, saved_logsum):
    rows, cols, width = queries.shape
    half = HEADS // 2
    split = half * HD
    tail = (half, HD)
    block = 4 * rows
    products = output_grad.astype(jnp.float32) * saved_output.astype(jnp.float32)
    delta_all = jnp.sum(products.reshape(rows, cols, HEADS, HD), axis=3)

    def row_group(values, last):
        return values.reshape((rows // SW, SW * values.shape[1]) + last)

    def column_group(values, last):
        count = values.shape[0]
        shaped = values.reshape((count, cols // SW, SW) + last)
        return jnp.swapaxes(shaped, 0, 1).reshape((cols // SW, count * SW) + last)

    def column_back(values, count):
        shaped = values.reshape((cols // SW, count, SW, -1))
        return jnp.swapaxes(shaped, 0, 1).reshape(count, cols, -1)

    full_key, full_value = (
        lax.all_gather(key_map[:, :, :split], "col", axis=1, tiled=True),
        lax.all_gather(value_map[:, :, :split], "col", axis=1, tiled=True),
    )
    wide = full_key.shape[1]
    stripe_query = row_group(queries[:, :, :split], tail)
    stripe_grad = row_group(output_grad[:, :, :split], tail)
    stripe_logsum = row_group(saved_logsum[:, :, :half], (half,))
    stripe_delta = row_group(delta_all[:, :, :half], (half,))
    stripe_key = row_group(full_key, tail)
    stripe_value = row_group(full_value, tail)
    probs_half, grad_scores = attention_terms(
        stripe_query, stripe_key, stripe_value, stripe_grad, stripe_logsum, stripe_delta
    )
    row_query_grad = query_side(grad_scores, stripe_key).reshape(rows, cols, split)
    row_key_part, row_value_part = key_side(probs_half, grad_scores, stripe_query, stripe_grad)
    row_term = jnp.concatenate(
        (row_key_part.reshape(rows, wide, split), row_value_part.reshape(rows, wide, split)), axis=2
    )
    row_sums = lax.psum_scatter(row_term, "col", scatter_dimension=1, tiled=True)
    local_key = key_map[:, :, split:]
    local_value = value_map[:, :, split:]
    column_query = column_group(queries[:, :, split:], tail)
    column_grad = column_group(output_grad[:, :, split:], tail)
    column_logsum = column_group(saved_logsum[:, :, half:], (half,))
    column_delta = column_group(delta_all[:, :, half:], (half,))

    def query_step(total, pieces):
        grouped_key = column_group(pieces[0], tail)
        grouped_value = column_group(pieces[1], tail)
        weights, gradients = attention_terms(
            column_query, grouped_key, grouped_value, column_grad, column_logsum, column_delta
        )
        return total + query_side(gradients, grouped_key)

    empty_query = jnp.zeros(column_query.shape, jnp.float32)
    every_key, every_value = (
        lax.all_gather(local_key, "row", axis=0, tiled=True),
        lax.all_gather(local_value, "row", axis=0, tiled=True),
    )
    column_total = in_blocks(query_step, empty_query, (every_key, every_value), block)

    def key_step(pieces):
        count = pieces[0].shape[0]
        grouped_key = column_group(pieces[0], tail)
        grouped_value = column_group(pieces[1], tail)
        weights, gradients = attention_terms(
            column_query, grouped_key, grouped_value, column_grad, column_logsum, column_delta
        )
        key_part, value_part = key_side(weights, gradients, column_query, column_grad)
        return jnp.concatenate(
            (column_back(key_part, count), column_back(value_part, count)), axis=2
        )

    count = rows * lax.axis_size("row")
    stacked = lax.map(
        key_step,
        (
            every_key.reshape((count // block, block) + every_key.shape[1:]),
            every_value.reshape((count // block, block) + every_value.shape[1:]),
        ),
    )
    column_sums = lax.psum_scatter(
        stacked.reshape((count,) + stacked.shape[2:]), "row", scatter_dimension=0, tiled=True
    )
    column_key_grad = column_sums[:, :, :split]
    column_value_grad = column_sums[:, :, split:]
    column_query_grad = column_back(column_total, rows)
    query_grad = jnp.concatenate((row_query_grad, column_query_grad), axis=2)
    key_grad = jnp.concatenate((row_sums[:, :, :split], column_key_grad), axis=2)
    value_grad = jnp.concatenate((row_sums[:, :, split:], column_value_grad), axis=2)
    return (query_grad, key_grad, value_grad)


def solution(mesh):
    in_specs = (
        P(("grp", "row"), "col", None),
        P(("grp", "row"), "col", None),
        P(("grp", "row"), "col", None),
        P(("grp", "row"), "col", None),
        P(("grp", "row"), "col", None),
        P(("grp", "row"), "col", None),
    )
    out_specs = (
        P(("grp", "row"), "col", None),
        P(("grp", "row"), "col", None),
        P(("grp", "row"), "col", None),
    )
    return jax.shard_map(local, mesh=mesh, in_specs=in_specs, out_specs=out_specs, check_vma=False)
```

profile of v0, /device:TPU:0, one launch (start us, length us, event | category | flops | bytes accessed | tf_op | source)
XLA Modules:
  0.0 230.9 jit_solution(451609579921056078)
XLA Ops:
  8.1 1.7 fusion.35
  9.8 1.6 fusion.33
  11.5 1.0 fusion.36
  12.5 1.0 fusion.38
  14.0 2.1 all_gather.12
  16.4 0.3 copy.102
  16.7 2.0 all_gather.13
  19.8 0.3 reduce_sum.9
  20.3 0.4 fusion.25
  20.7 0.4 fusion.26
  21.1 0.8 copy-done.6
  22.1 0.4 copy.117
  23.0 0.4 copy.119
  23.7 1.1 pad_maximum_fusion
  26.3 28.2 %all-gather.3.cloned.1.call-done = bf16[64,16,512]{2,1,0:T(8,128)(2,1)} async-done(((bf16[8,16,512]{2,1,0:T(8,128)(2,1)}), bf16[64,16,512]{2,1,0:T(8,128)(2,1)}) %all-gather.3.cloned.1.call-update) | async-done | bytes 1048592 | tf_op jit(solution)/shard_map/all_gather | solution.py:115
  54.5 41.1 %all-gather.5.cloned.1.call-done = bf16[64,16,512]{2,1,0:T(8,128)(2,1)} async-done(((bf16[8,16,512]{2,1,0:T(8,128)(2,1)}), bf16[64,16,512]{2,1,0:T(8,128)(2,1)}) %all-gather.5.cloned.1.call-update) | async-done | bytes 1048592 | tf_op jit(solution)/shard_map/all_gather | solution.py:116
  95.6 38.5 %while.24 = (s32[]{:T(128)}, f32[2,32,16,1024]{3,2,1,0:T(8,128)}, bf16[2,32,16,512]{3,2,1,0:T(8,128)(2,1)}, bf16[2,64,8,64]{1,3,2,0:T(8,128)(2,1)S(1)}, f32[2,64...) while((s32[]{:T(128)}, f32[2,32,16,1024]{3,2,1,0:T(8,128)}, ...), condition=%wide.region_5.6_spmd, body=%wide.region_4.5_spmd.sunk | while | flops 136577024 | bytes 35135680 | solution.py:133
  95.6 2.2 constant_dynamic-slice_fusion.6
  97.7 0.5 reshape.208
  98.3 0.5 fusion.85
  98.9 1.4 convolution_bitcast_fusion.3
  100.3 2.0 copy.157
  102.3 1.6 reshape.209
  103.8 2.4 %copy_bitcast_fusion.7 = f32[32,16,512]{2,1,0:T(8,128)} fusion(f32[2,32,8,512]{3,2,1,0:T(8,128)} %reshape.209), kind=kLoop, calls=%fused_computation.11.clone.1 | loop fusion | bytes 2097152 | tf_op jit(solution)/shard_map/while/body/eval_jaxpr/reshape | solution.py:76
  106.2 1.6 reshape.210
  108.0 1.6 fusion.86
  109.6 0.8 copy.159
  110.4 1.6 reshape.211
  112.0 1.3 copy_bitcast_fusion.8
  113.3 1.5 fusion.87
  114.8 2.2 constant_dynamic-slice_fusion.6
  117.0 0.5 reshape.208
  117.6 0.5 fusion.85
  118.1 1.4 convolution_bitcast_fusion.3
  119.5 2.0 copy.157
  121.5 1.6 reshape.209
  123.1 2.4 %copy_bitcast_fusion.7 = f32[32,16,512]{2,1,0:T(8,128)} fusion(f32[2,32,8,512]{3,2,1,0:T(8,128)} %reshape.209), kind=kLoop, calls=%fused_computation.11.clone.1 | loop fusion | bytes 2097152 | tf_op jit(solution)/shard_map/while/body/eval_jaxpr/reshape | solution.py:76
  125.5 1.6 reshape.210
  127.2 1.6 fusion.86
  128.9 0.8 copy.159
  129.7 1.6 reshape.211
  131.2 1.3 copy_bitcast_fusion.8
  132.6 1.5 fusion.87
  134.1 1.0 copy-done.7
  135.7 0.9 reshape.182
  136.6 10.4 %while.25 = (s32[]{:T(128)}, f32[2,64,8,64]{1,3,2,0:T(8,128)S(1)}, bf16[64,16,512]{2,1,0:T(8,128)(2,1)}, bf16[2,64,8,64]{3,1,2,0:T(8,128)(2,1)}, f32[2,64,8]{1,2...) while((s32[]{:T(128)}, f32[2,64,8,64]{1,3,2,0:T(8,128)S(1)}, ...), condition=%wide.region_2.0_spmd.clone, body=%wide.region_1.0_spmd.clone.sunk | while | flops 102170624 | bytes 11280569 | solution.py:54
  136.6 1.3 constant_dynamic-slice_fusion.7
  137.8 0.5 reshape.212
  138.5 0.6 copy.162
  139.1 0.5 reshape.213
  139.7 0.5 convolution_subtract_fusion.4
  140.2 1.6 fusion.93
  141.8 1.3 constant_dynamic-slice_fusion.7
  143.0 0.5 reshape.212
  143.7 0.6 copy.162
  144.3 0.5 reshape.213
  144.9 0.5 convolution_subtract_fusion.4
  145.4 1.6 fusion.93
  147.4 1.8 pad_maximum_fusion.1
  149.2 1.1 fusion.31
  150.2 70.5 %reduce-scatter.5.cloned.1.call-done = f32[8,16,1024]{2,1,0:T(8,128)} async-done(((f32[64,16,1024]{2,1,0:T(8,128)}), f32[8,16,1024]{2,1,0:T(8,128)}) %reduce-scatter.5.cloned.1.call-update) | async-done | bytes 524304 | tf_op jit(solution)/shard_map/reduce_scatter | solution.py:140
  220.7 1.1 fusion.32
  221.8 0.8 pad_maximum_fusion.3
  222.6 0.8 pad_maximum_fusion.2
  (78 shorter events, 6.1 us)
Async XLA Ops:
  8.0 11.0 %copy-start.10 = (bf16[8,16,1024]{2,1,0:T(8,128)(2,1)S(1)}, bf16[8,16,1024]{2,1,0:T(8,128)(2,1)}, u32[]{:S(2)}) copy-start(bf16[8,16,1024]{2,1,0:T(8,128)(2,1)} %param.14) | copy-start | bytes 786436
  8.0 11.4 %copy-start.11 = (bf16[8,16,1024]{2,1,0:T(8,128)(2,1)S(1)}, bf16[8,16,1024]{2,1,0:T(8,128)(2,1)}, u32[]{:S(2)}) copy-start(bf16[8,16,1024]{2,1,0:T(8,128)(2,1)} %param.13) | copy-start | bytes 786436
  8.0 46.5 %all-gather.3.cloned.1.call-start = ((), (), s32[]{:S(2)}) async-start(), calls=%async_computation.2 | async-start | bytes 1179648 | tf_op jit(solution)/shard_map/all_gather | solution.py:115
  9.8 85.8 %all-gather.5.cloned.1.call-start = ((), (), s32[]{:S(2)}) async-start(), calls=%async_computation.3 | async-start | bytes 1179648 | tf_op jit(solution)/shard_map/all_gather | solution.py:116
  11.5 137.7 %reduce-scatter.3.cloned.1.call-start = ((), (), s32[]{:S(2)}) async-start(), calls=%async_computation.4 | async-start | bytes 1572864 | tf_op jit(solution)/shard_map/reduce_scatter | solution.py:97
  16.7 4.3 %copy-start.8 = (bf16[256,8,64]{0,2,1:T(8,128)(2,1)}, bf16[256,8,64]{0,2,1:T(8,128)(2,1)S(1)}, u32[]{:S(2)}) copy-start(bf16[256,8,64]{0,2,1:T(8,128)(2,1)S(1)} %copy.102) | copy-start | bytes 786436
  21.0 0.8 copy-start.6
  24.8 196.0 %reduce-scatter.5.cloned.1.call-start = ((), (), s32[]{:S(2)}) async-start(), calls=%async_computation.5 | async-start | bytes 4718592 | tf_op jit(solution)/shard_map/reduce_scatter | solution.py:140
  25.7 69.9 %copy-start.3 = (bf16[2,64,8,64]{3,1,2,0:T(8,128)(2,1)}, bf16[2,64,8,64]{3,1,2,0:T(8,128)(2,1)S(1)}, u32[]{:S(2)}) copy-start(bf16[2,64,8,64]{3,1,2,0:T(8,128)(2,1)S(1)} %get-tuple-element.411) | copy-start | bytes 393220
  25.7 69.9 %copy-start.5 = (bf16[2,64,8,64]{3,1,2,0:T(8,128)(2,1)}, bf16[2,64,8,64]{3,1,2,0:T(8,128)(2,1)S(1)}, u32[]{:S(2)}) copy-start(bf16[2,64,8,64]{3,1,2,0:T(8,128)(2,1)S(1)} %get-tuple-element.408) | copy-start | bytes 393220
  95.6 3.3 %copy-start.1 = (bf16[2,64,8,64]{1,3,2,0:T(8,128)(2,1)}, bf16[2,64,8,64]{1,3,2,0:T(8,128)(2,1)S(1)}, u32[]{:S(2)}) copy-start(bf16[2,64,8,64]{1,3,2,0:T(8,128)(2,1)S(1)} %get-tuple-element.462) | copy-start | bytes 393220 | tf_op jit(solution)/shard_map/while
  110.4 2.9 %copy-start = (f32[32,16,512]{2,1,0:T(8,128)S(1)}, f32[32,16,512]{2,1,0:T(8,128)}, u32[]{:S(2)}) copy-start(f32[32,16,512]{2,1,0:T(8,128)} %copy_bitcast_fusion.7) | copy-start | bytes 3145732 | tf_op jit(solution)/shard_map/while
  112.0 2.9 %copy-start.2 = (bf16[2,64,8,64]{1,3,2,0:T(8,128)(2,1)S(1)}, bf16[2,64,8,64]{1,3,2,0:T(8,128)(2,1)}, u32[]{:S(2)}) copy-start(bf16[2,64,8,64]{1,3,2,0:T(8,128)(2,1)} %copy-done.1) | copy-start | bytes 393220 | tf_op jit(solution)/shard_map/while
  114.8 3.3 %copy-start.1 = (bf16[2,64,8,64]{1,3,2,0:T(8,128)(2,1)}, bf16[2,64,8,64]{1,3,2,0:T(8,128)(2,1)S(1)}, u32[]{:S(2)}) copy-start(bf16[2,64,8,64]{1,3,2,0:T(8,128)(2,1)S(1)} %get-tuple-element.462) | copy-start | bytes 393220 | tf_op jit(solution)/shard_map/while
  129.6 2.9 %copy-start = (f32[32,16,512]{2,1,0:T(8,128)S(1)}, f32[32,16,512]{2,1,0:T(8,128)}, u32[]{:S(2)}) copy-start(f32[32,16,512]{2,1,0:T(8,128)} %copy_bitcast_fusion.7) | copy-start | bytes 3145732 | tf_op jit(solution)/shard_map/while
  131.2 2.8 %copy-start.2 = (bf16[2,64,8,64]{1,3,2,0:T(8,128)(2,1)S(1)}, bf16[2,64,8,64]{1,3,2,0:T(8,128)(2,1)}, u32[]{:S(2)}) copy-start(bf16[2,64,8,64]{1,3,2,0:T(8,128)(2,1)} %copy-done.1) | copy-start | bytes 393220 | tf_op jit(solution)/shard_map/while
  134.0 1.0 copy-start.7
  134.0 1.1 copy-start.9
  134.0 2.5 %copy-start.4 = (bf16[2,64,8,64]{3,1,2,0:T(8,128)(2,1)S(1)}, bf16[2,64,8,64]{3,1,2,0:T(8,128)(2,1)}, u32[]{:S(2)}) copy-start(bf16[2,64,8,64]{3,1,2,0:T(8,128)(2,1)} %copy-done.3) | copy-start | bytes 393220
Sparse Core Ops, SparseCore 0:
  11.6 42.9 all-gather.2
  56.6 38.8 all-gather.4
Sparse Core Ops, SparseCore 1:
  24.8 11.1 reduce-scatter.2
  134.2 86.5 reduce-scatter.4
where the time goes:
time: 232 us; the launch traced here: 231 us
  waiting for transfers between devices  140 us (60%)
  local copies, waits for them, and re-layouts  49.9 us (22%)
  between operations  15.8 us (7%)
  matrix products  12.7 us (5%)
  other arithmetic  7.9 us (3%)
  blocking collectives  4.08 us (2%)
    reduce_scatter x1, waiting for transfers between devices, local(): lax.psum_scatter(stacked.reshape((count,) + stacked.shape[2:]), 'row', sc...  70.5 us
    all_gather x1, waiting for transfers between devices, local(): lax.all_gather(local_value, 'row', axis=0, tiled=True)  41.1 us
    all_gather x1, waiting for transfers between devices, local(): lax.all_gather(local_key, 'row', axis=0, tiled=True)  28.2 us
    reshape x5, local copies, waits for them, and re-layouts, column_back(): return jnp.swapaxes(shaped, 0, 1).reshape(count, cols, -1)  7.5 us
    reshape x12, local copies, waits for them, and re-layouts, column_group(): shaped = values.reshape((count, cols // SW, SW) + last)  7.02 us
    reshape x5, local copies, waits for them, and re-layouts, column_back(): shaped = values.reshape((cols // SW, count, SW, -1))  6.37 us
  transfers between devices with their start and end apart: 4, of which 3 were waited for; matrix products, arithmetic and copies ran while one was open for 28% of the time, Pallas kernels for 0%

commit v1 on v0

--- a/solution.py
+++ b/solution.py
@@ -7,6 +7,19 @@
 HEADS = 16
 HD = 64
 SW = 8
+
+
+def ring_gather(value, axis, dim):
+    ways = lax.axis_size(axis)
+    up = [(d, (d + 1) % ways) for d in range(ways)]
+    down = [(d, (d - 1) % ways) for d in range(ways)]
+    earlier, later = ([value], [value])
+    for _ in range(ways // 2):
+        earlier.append(lax.ppermute(earlier[-1], axis, up))
+    for _ in range((ways - 1) // 2):
+        later.append(lax.ppermute(later[-1], axis, down))
+    line = jnp.concatenate([*earlier[::-1], *later[1:]], axis=dim)
+    return jnp.roll(line, (lax.axis_index(axis) - ways // 2) * value.shape[dim], axis=dim)
 
 
 def attention_terms(
@@ -113,7 +126,7 @@
     empty_query = jnp.zeros(column_query.shape, jnp.float32)
     every_key, every_value = (
         lax.all_gather(local_key, "row", axis=0, tiled=True),
-        lax.all_gather(local_value, "row", axis=0, tiled=True),
+        ring_gather(local_value, "row", 0),
     )
     column_total = in_blocks(query_step, empty_query, (every_key, every_value), block)
 

time: 232 us -> 209 us (0.901)
  waiting for transfers between devices: 140 us -> 87 us
  starting transfers between devices: 0.35 us -> 16.3 us
  local copies, waits for them, and re-layouts: 49.9 us -> 64.3 us
    all_gather x1 -> x0, waiting for transfers between devices: 41.1 us -> none  [local(): lax.all_gather(local_value, 'row', axis=0, tiled=True)]
    all_gather x1, waiting for transfers between devices: 28.2 us -> 0.01 us  [local(): lax.all_gather(local_key, 'row', axis=0, tiled=True)]
    ppermute x0 -> x7, waiting for transfers between devices: none -> 16.3 us  [the longest x4 14.6 us: ring_gather(): earlier.append(lax.ppermute(earlier[-1], axis, up))]
    ppermute x0 -> x7, starting transfers between devices: none -> 16 us  [the longest x3 15.9 us: ring_gather(): later.append(lax.ppermute(later[-1], axis, down))]
    unnamed x18 -> x46, local copies, waits for them, and re-layouts: 1.88 us -> 13.4 us
  transfers between devices with their start and end apart: 4 -> 10, of which waited for: 3 -> 5; matrix products, arithmetic and copies ran while one was open for 28% -> 36% of each run, Pallas kernels for 0% -> 0%
where the time goes in v1:
time: 209 us; the launch traced here: 208 us
  waiting for transfers between devices  87 us (42%)
  local copies, waits for them, and re-layouts  64.3 us (31%)
  starting transfers between devices  16.3 us (8%)
  between operations  16.1 us (8%)
  matrix products  12.8 us (6%)
  other arithmetic  7.11 us (3%)
  blocking collectives  3.98 us (2%)
    reduce_scatter x1, waiting for transfers between devices, local(): lax.psum_scatter(stacked.reshape((count,) + stacked.shape[2:]), 'row', sc...  70.6 us
    ppermute x3, starting transfers between devices, ring_gather(): later.append(lax.ppermute(later[-1], axis, down))  15.9 us
    ppermute x4, waiting for transfers between devices, ring_gather(): earlier.append(lax.ppermute(earlier[-1], axis, up))  14.6 us
    unnamed x46, local copies, waits for them, and re-layouts  13.4 us
    reshape x5, local copies, waits for them, and re-layouts, column_back(): return jnp.swapaxes(shaped, 0, 1).reshape(count, cols, -1)  7.39 us
    reshape x5, local copies, waits for them, and re-layouts, column_back(): shaped = values.reshape((cols // SW, count, SW, -1))  6.08 us
    reshape x12, local copies, waits for them, and re-layouts, column_group(): shaped = values.reshape((count, cols // SW, SW) + last)  4.8 us
    transpose x3, local copies, waits for them, and re-layouts, key_side(): jnp.einsum('ghab,gahe->gbhe', probs_half, stripe_grad, preferred_element_...  4.44 us
  transfers between devices with their start and end apart: 10, of which 5 were waited for; matrix products, arithmetic and copies ran while one was open for 36% of the time, Pallas kernels for 0%

profile of v1, /device:TPU:0, one launch (start us, length us, event | category | flops | bytes accessed | tf_op | source)
XLA Modules:
  0.0 207.9 jit_solution(8476054584824247530)
XLA Ops:
  8.0 1.6 slice.57
  9.6 6.0 %collective-permute-start.4 = (bf16[8,16,512]{2,1,0:T(8,128)(2,1)}, bf16[8,16,512]{2,1,0:T(8,128)(2,1)}, u32[]{:S(2)}, u32[]{:S(2)}) collective-permute-start(bf16[8,16,512]{2,1,0:T(8,128)(2,1)} %slice.57), channel_id=1, source_target_pairs={{0,14},{2,0},{4,2},{6,4},{8,6},{10,8},{12,10},{14,12},{1,15},{3,1}... | collective-permute-start | bytes 393224 | tf_op jit(solution)/shard_map/ppermute | solution.py:20
  15.6 1.6 fusion.35
  17.4 1.0 fusion.38
  18.4 0.7 copy.103
  19.2 1.0 fusion.36
  20.8 2.0 all_gather.9
  23.7 0.8 copy.104
  26.1 0.7 copy.124
  27.0 10.5 %collective-permute-done.1 = bf16[8,16,512]{2,1,0:T(8,128)(2,1)S(1)} collective-permute-done((bf16[8,16,512]{2,1,0:T(8,128)(2,1)}, bf16[8,16,512]{2,1,0:T(8,128)(2,1)S(1)}, u32[]{:S(2)}, u32[]{:S(2)}) %collective-permute-start.1) | collective-permute-done | bytes 131104 | tf_op jit(solution)/shard_map/ppermute | solution.py:18
  37.5 1.1 fusion.25
  38.6 4.8 %collective-permute-start.5 = (bf16[8,16,512]{2,1,0:T(8,128)(2,1)}, bf16[8,16,512]{2,1,0:T(8,128)(2,1)S(1)}, u32[]{:S(2)}, u32[]{:S(2)}) collective-permute-start(bf16[8,16,512]{2,1,0:T(8,128)(2,1)} %collective-permute-done.4), channel_id=1, source_target_pairs={{0,14},{2,0},{4,2},{6,4},{8,6},{10,8},{12,10},{14,12},{1,15},{3,1}... | collective-permute-start | bytes 393224 | tf_op jit(solution)/shard_map/ppermute | solution.py:20
  43.3 2.0 collective-permute-done.2
  45.3 1.1 convolution_bitcast_fusion.1
  47.2 1.8 collective-permute-done.5
  48.9 5.1 %collective-permute-start.6 = (bf16[8,16,512]{2,1,0:T(8,128)(2,1)S(1)}, bf16[8,16,512]{2,1,0:T(8,128)(2,1)S(1)}, u32[]{:S(2)}, u32[]{:S(2)}) collective-permute-start(bf16[8,16,512]{2,1,0:T(8,128)(2,1)S(1)} %collective-permute-done.5), channel_id=1, source_target_pairs={{0,14},{2,0},{4,2},{6,4},{8,6},{10,8},{12,10},{14,12},{1,15},{3,1}... | collective-permute-start | bytes 393224 | tf_op jit(solution)/shard_map/ppermute | solution.py:20
  54.1 2.1 collective-permute-done.3
  56.2 0.9 constant_dynamic-update-slice_fusion.15
  57.1 0.9 constant_dynamic-update-slice_fusion.14
  58.0 0.9 constant_dynamic-update-slice_fusion.12
  59.0 0.9 constant_dynamic-update-slice_fusion.11
  59.9 0.9 constant_dynamic-update-slice_fusion.10
  60.9 0.9 constant_dynamic-update-slice_fusion.7
  61.8 0.9 constant_dynamic-update-slice_fusion.6
  62.7 0.9 constant_dynamic-update-slice_fusion.4
  63.7 1.4 copy-done.16
  65.1 2.0 all_gather.10
  67.3 1.0 fusion.26
  68.4 0.8 copy-done.8
  70.1 1.2 pad_maximum_fusion
  71.5 1.6 constant_dynamic-update-slice_fusion.2
  74.4 2.3 %constant_dynamic-slice_fusion.4 = bf16[64,16,512]{2,1,0:T(8,128)(2,1)} fusion(bf16[128,16,512]{2,1,0:T(8,128)(2,1)} %constant_dynamic-update-slice_fusion, s32[]{:T(128)S(6)} %select_n.22), kind=kLoop, calls=%fused_computation.74 | loop fusion | bytes 2097156 | tf_op jit(solution)/shard_map/jit(_roll_dynamic)/dynamic_slice | solution.py:22
  76.7 35.8 %while.24 = (s32[]{:T(128)}, f32[2,32,16,1024]{3,2,1,0:T(8,128)}, bf16[2,32,16,512]{3,2,1,0:T(8,128)(2,1)}, bf16[2,64,8,64]{1,3,2,0:T(8,128)(2,1)S(1)}, f32[2,64...) while((s32[]{:T(128)}, f32[2,32,16,1024]{3,2,1,0:T(8,128)}, ...), condition=%wide.region_5.6_spmd, body=%wide.region_4.5_spmd.sunk | while | flops 136577024 | bytes 37232860 | solution.py:146
  76.7 2.2 %constant_dynamic-slice_fusion.7 = (bf16[1,32,16,512]{3,2,1,0:T(8,128)(2,1)}, bf16[1,32,16,512]{3,2,1,0:T(8,128)(2,1)S(1)}) fusion(bf16[2,32,16,512]{3,2,1,0:T(8,128)(2,1)} %get-tuple-element.464, s32[]{:T(128)S(6)} %copy.188, bf16[2,32,16,512]{3,2,1,0:T(8,128)(2,1)} %get-tuple-element.461), kind=kLoop, calls=%fused_computation.17.clone.1 | loop fusion | bytes 2097156 | tf_op jit(solution)/shard_map/while/body/jit(dynamic_index_in_dim)/dynamic_slice | solution.py:146
  80.1 1.3 convolution_bitcast_fusion.3
  81.4 2.0 copy.157
  83.4 1.5 reshape.209
  84.9 2.4 %copy_bitcast_fusion.7 = f32[32,16,512]{2,1,0:T(8,128)} fusion(f32[2,32,8,512]{3,2,1,0:T(8,128)} %reshape.209), kind=kLoop, calls=%fused_computation.11.clone.1 | loop fusion | bytes 2097152 | tf_op jit(solution)/shard_map/while/body/eval_jaxpr/reshape | solution.py:89
  87.9 1.6 fusion.86
  89.5 0.8 copy.159
  90.3 1.5 reshape.211
  91.8 1.3 copy_bitcast_fusion.8
  93.1 1.5 fusion.87
  94.6 2.2 %constant_dynamic-slice_fusion.7 = (bf16[1,32,16,512]{3,2,1,0:T(8,128)(2,1)}, bf16[1,32,16,512]{3,2,1,0:T(8,128)(2,1)S(1)}) fusion(bf16[2,32,16,512]{3,2,1,0:T(8,128)(2,1)} %get-tuple-element.464, s32[]{:T(128)S(6)} %copy.188, bf16[2,32,16,512]{3,2,1,0:T(8,128)(2,1)} %get-tuple-element.461), kind=kLoop, calls=%fused_computation.17.clone.1 | loop fusion | bytes 2097156 | tf_op jit(solution)/shard_map/while/body/jit(dynamic_index_in_dim)/dynamic_slice | solution.py:146
  97.9 1.3 convolution_bitcast_fusion.3
  99.2 2.0 copy.157
  101.3 1.5 reshape.209
  102.7 2.4 %copy_bitcast_fusion.7 = f32[32,16,512]{2,1,0:T(8,128)} fusion(f32[2,32,8,512]{3,2,1,0:T(8,128)} %reshape.209), kind=kLoop, calls=%fused_computation.11.clone.1 | loop fusion | bytes 2097152 | tf_op jit(solution)/shard_map/while/body/eval_jaxpr/reshape | solution.py:89
  105.8 1.6 fusion.86
  107.4 0.8 copy.159
  108.2 1.5 reshape.211
  109.7 1.3 copy_bitcast_fusion.8
  111.0 1.5 fusion.87
  112.5 1.0 copy-done.9
  114.1 0.9 reshape.182
  115.0 9.3 %while.25 = (s32[]{:T(128)}, f32[2,64,8,64]{1,3,2,0:T(8,128)S(1)}, bf16[64,16,512]{2,1,0:T(8,128)(2,1)}, bf16[2,64,8,64]{3,1,2,0:T(8,128)(2,1)}, f32[2,64,8]{1,2...) while((s32[]{:T(128)}, f32[2,64,8,64]{1,3,2,0:T(8,128)S(1)}, ...), condition=%wide.region_2.3_spmd.clone, body=%wide.region_1.0_spmd.clone.sunk | while | flops 102170624 | bytes 11804885 | solution.py:67
  115.0 1.3 constant_dynamic-slice_fusion.8
  119.7 1.3 constant_dynamic-slice_fusion.8
  125.3 0.8 pad_maximum_fusion.1
  126.1 1.1 fusion.31
  127.2 70.6 %reduce-scatter.5.cloned.1.call-done = f32[8,16,1024]{2,1,0:T(8,128)} async-done(((f32[64,16,1024]{2,1,0:T(8,128)}), f32[8,16,1024]{2,1,0:T(8,128)}) %reduce-scatter.5.cloned.1.call-update) | async-done | bytes 524304 | tf_op jit(solution)/shard_map/reduce_scatter | solution.py:153
  197.8 1.1 fusion.32
  198.8 0.8 pad_maximum_fusion.3
  199.7 0.8 pad_maximum_fusion.2
  (128 shorter events, 18.5 us)
Async XLA Ops:
  8.0 68.7 %all-gather.2.cloned.1.call-start = ((), (), s32[]{:S(2)}) async-start(), calls=%async_computation.2 | async-start | bytes 1179648 | tf_op jit(solution)/shard_map/all_gather | solution.py:128
  9.6 29.0 %collective-permute-start.4 = (bf16[8,16,512]{2,1,0:T(8,128)(2,1)}, bf16[8,16,512]{2,1,0:T(8,128)(2,1)}, u32[]{:S(2)}, u32[]{:S(2)}) collective-permute-start(bf16[8,16,512]{2,1,0:T(8,128)(2,1)} %slice.57), channel_id=1, source_target_pairs={{0,14},{2,0},{4,2},{6,4},{8,6},{10,8},{12,10},{14,12},{1,15},{3,1}... | collective-permute-start | bytes 393224 | tf_op jit(solution)/shard_map/ppermute | solution.py:20
  15.6 10.3 %collective-permute-start = (bf16[8,16,512]{2,1,0:T(8,128)(2,1)}, bf16[8,16,512]{2,1,0:T(8,128)(2,1)}, u32[]{:S(2)}, u32[]{:S(2)}) collective-permute-start(bf16[8,16,512]{2,1,0:T(8,128)(2,1)} %slice.57), channel_id=1, source_target_pairs={{0,2},{2,4},{4,6},{6,8},{8,10},{10,12},{12,14},{14,0},{1,3},{3,5},... | collective-permute-start | bytes 393224 | tf_op jit(solution)/shard_map/ppermute | solution.py:18
  17.3 108.8 %reduce-scatter.3.cloned.1.call-start = ((), (), s32[]{:S(2)}) async-start(), calls=%async_computation.3 | async-start | bytes 1572864 | tf_op jit(solution)/shard_map/reduce_scatter | solution.py:110
  17.4 6.0 %copy-start.15 = (bf16[8,16,1024]{2,1,0:T(8,128)(2,1)S(1)}, bf16[8,16,1024]{2,1,0:T(8,128)(2,1)}, u32[]{:S(2)}) copy-start(bf16[8,16,1024]{2,1,0:T(8,128)(2,1)} %param.14) | copy-start | bytes 786436
  23.4 14.1 %copy-start.10 = (bf16[256,8,64]{0,2,1:T(8,128)(2,1)}, bf16[256,8,64]{0,2,1:T(8,128)(2,1)S(1)}, u32[]{:S(2)}) copy-start(bf16[256,8,64]{0,2,1:T(8,128)(2,1)S(1)} %copy.102) | copy-start | bytes 786436
  23.4 1.8 copy-start.20
  24.8 1.1 copy-start.4
  24.8 1.1 copy-start.6
  25.9 11.5 %collective-permute-start.1 = (bf16[8,16,512]{2,1,0:T(8,128)(2,1)}, bf16[8,16,512]{2,1,0:T(8,128)(2,1)S(1)}, u32[]{:S(2)}, u32[]{:S(2)}) collective-permute-start(bf16[8,16,512]{2,1,0:T(8,128)(2,1)} %collective-permute-done), channel_id=1, source_target_pairs={{0,2},{2,4},{4,6},{6,8},{8,10},{10,12},{12,14},{14,0},{1,3},{3,5},... | collective-permute-start | bytes 393224 | tf_op jit(solution)/shard_map/ppermute | solution.py:18
  37.5 7.8 %copy-start.17 = (bf16[8,16,512]{2,1,0:T(8,128)(2,1)}, bf16[8,16,512]{2,1,0:T(8,128)(2,1)S(1)}, u32[]{:S(2)}) copy-start(bf16[8,16,512]{2,1,0:T(8,128)(2,1)S(1)} %collective-permute-done.1) | copy-start | bytes 393220
  37.5 7.8 %collective-permute-start.2 = (bf16[8,16,512]{2,1,0:T(8,128)(2,1)S(1)}, bf16[8,16,512]{2,1,0:T(8,128)(2,1)}, u32[]{:S(2)}, u32[]{:S(2)}) collective-permute-start(bf16[8,16,512]{2,1,0:T(8,128)(2,1)S(1)} %collective-permute-done.1), channel_id=1, source_target_pairs={{0,2},{2,4},{4,6},{6,8},{8,10},{10,12},{12,14},{14,0},{1,3},{3,5},... | collective-permute-start | bytes 393224 | tf_op jit(solution)/shard_map/ppermute | solution.py:18
  38.6 10.4 %collective-permute-start.5 = (bf16[8,16,512]{2,1,0:T(8,128)(2,1)}, bf16[8,16,512]{2,1,0:T(8,128)(2,1)S(1)}, u32[]{:S(2)}, u32[]{:S(2)}) collective-permute-start(bf16[8,16,512]{2,1,0:T(8,128)(2,1)} %collective-permute-done.4), channel_id=1, source_target_pairs={{0,14},{2,0},{4,2},{6,4},{8,6},{10,8},{12,10},{14,12},{1,15},{3,1}... | collective-permute-start | bytes 393224 | tf_op jit(solution)/shard_map/ppermute | solution.py:20
  45.3 10.8 %collective-permute-start.3 = (bf16[8,16,512]{2,1,0:T(8,128)(2,1)}, bf16[8,16,512]{2,1,0:T(8,128)(2,1)}, u32[]{:S(2)}, u32[]{:S(2)}) collective-permute-start(bf16[8,16,512]{2,1,0:T(8,128)(2,1)} %collective-permute-done.2), channel_id=1, source_target_pairs={{0,2},{2,4},{4,6},{6,8},{8,10},{10,12},{12,14},{14,0},{1,3},{3,5},... | collective-permute-start | bytes 393224 | tf_op jit(solution)/shard_map/ppermute | solution.py:18
  46.4 11.5 %copy-start.18 = (bf16[8,16,512]{2,1,0:T(8,128)(2,1)S(1)}, bf16[8,16,512]{2,1,0:T(8,128)(2,1)}, u32[]{:S(2)}) copy-start(bf16[8,16,512]{2,1,0:T(8,128)(2,1)} %copy-done.17) | copy-start | bytes 393220
  47.2 15.5 %copy-start.19 = (bf16[8,16,512]{2,1,0:T(8,128)(2,1)S(1)}, bf16[8,16,512]{2,1,0:T(8,128)(2,1)}, u32[]{:S(2)}) copy-start(bf16[8,16,512]{2,1,0:T(8,128)(2,1)} %copy-done.17) | copy-start | bytes 393220
  47.2 16.5 %copy-start.13 = (bf16[8,16,1024]{2,1,0:T(8,128)(2,1)S(1)}, bf16[8,16,1024]{2,1,0:T(8,128)(2,1)}, u32[]{:S(2)}) copy-start(bf16[8,16,1024]{2,1,0:T(8,128)(2,1)} %param.12) | copy-start | bytes 786436
  48.9 11.9 %collective-permute-start.6 = (bf16[8,16,512]{2,1,0:T(8,128)(2,1)S(1)}, bf16[8,16,512]{2,1,0:T(8,128)(2,1)S(1)}, u32[]{:S(2)}, u32[]{:S(2)}) collective-permute-start(bf16[8,16,512]{2,1,0:T(8,128)(2,1)S(1)} %collective-permute-done.5), channel_id=1, source_target_pairs={{0,14},{2,0},{4,2},{6,4},{8,6},{10,8},{12,10},{14,12},{1,15},{3,1}... | collective-permute-start | bytes 393224 | tf_op jit(solution)/shard_map/ppermute | solution.py:20
  58.0 9.3 %copy-start.12 = (bf16[128,8,64]{0,2,1:T(8,128)(2,1)S(1)}, bf16[128,8,64]{0,2,1:T(8,128)(2,1)}, u32[]{:S(2)}) copy-start(bf16[128,8,64]{0,2,1:T(8,128)(2,1)} %copy.104) | copy-start | bytes 393220
  63.7 1.4 copy-start.16
  68.4 0.8 copy-start.8
  71.3 126.5 %reduce-scatter.5.cloned.1.call-start = ((), (), s32[]{:S(2)}) async-start(), calls=%async_computation.4 | async-start | bytes 4718592 | tf_op jit(solution)/shard_map/reduce_scatter | solution.py:153
  76.7 3.3 %copy-start.2 = (bf16[2,64,8,64]{1,3,2,0:T(8,128)(2,1)}, bf16[2,64,8,64]{1,3,2,0:T(8,128)(2,1)S(1)}, u32[]{:S(2)}) copy-start(bf16[2,64,8,64]{1,3,2,0:T(8,128)(2,1)S(1)} %get-tuple-element.462) | copy-start | bytes 393220 | tf_op jit(solution)/shard_map/while
  84.9 2.4 %copy-start.1 = (bf16[1,32,16,512]{3,2,1,0:T(8,128)(2,1)S(1)}, bf16[1,32,16,512]{3,2,1,0:T(8,128)(2,1)}, u32[]{:S(2)}) copy-start(bf16[1,32,16,512]{3,2,1,0:T(8,128)(2,1)} %get-tuple-element.394) | copy-start | bytes 1572868 | tf_op jit(solution)/shard_map/while
  90.3 2.8 %copy-start = (f32[32,16,512]{2,1,0:T(8,128)S(1)}, f32[32,16,512]{2,1,0:T(8,128)}, u32[]{:S(2)}) copy-start(f32[32,16,512]{2,1,0:T(8,128)} %copy_bitcast_fusion.7) | copy-start | bytes 3145732 | tf_op jit(solution)/shard_map/while
  93.1 1.5 copy-start.3
  94.6 3.3 %copy-start.2 = (bf16[2,64,8,64]{1,3,2,0:T(8,128)(2,1)}, bf16[2,64,8,64]{1,3,2,0:T(8,128)(2,1)S(1)}, u32[]{:S(2)}) copy-start(bf16[2,64,8,64]{1,3,2,0:T(8,128)(2,1)S(1)} %get-tuple-element.462) | copy-start | bytes 393220 | tf_op jit(solution)/shard_map/while
  102.7 2.4 %copy-start.1 = (bf16[1,32,16,512]{3,2,1,0:T(8,128)(2,1)S(1)}, bf16[1,32,16,512]{3,2,1,0:T(8,128)(2,1)}, u32[]{:S(2)}) copy-start(bf16[1,32,16,512]{3,2,1,0:T(8,128)(2,1)} %get-tuple-element.394) | copy-start | bytes 1572868 | tf_op jit(solution)/shard_map/while
  108.2 2.8 %copy-start = (f32[32,16,512]{2,1,0:T(8,128)S(1)}, f32[32,16,512]{2,1,0:T(8,128)}, u32[]{:S(2)}) copy-start(f32[32,16,512]{2,1,0:T(8,128)} %copy_bitcast_fusion.7) | copy-start | bytes 3145732 | tf_op jit(solution)/shard_map/while
  111.0 1.5 copy-start.3
  112.5 1.0 copy-start.9
  112.5 1.1 copy-start.11
  112.5 2.5 %copy-start.5 = (bf16[2,64,8,64]{3,1,2,0:T(8,128)(2,1)S(1)}, bf16[2,64,8,64]{3,1,2,0:T(8,128)(2,1)}, u32[]{:S(2)}) copy-start(bf16[2,64,8,64]{3,1,2,0:T(8,128)(2,1)} %copy-done.4) | copy-start | bytes 393220
  118.0 1.0 copy-start.7
  122.7 1.0 copy-start.7
  124.3 1.0 copy-start.14
Sparse Core Ops, SparseCore 0:
  17.4 46.3 all-gather.1
Sparse Core Ops, SparseCore 1:
  71.4 5.8 reduce-scatter.2
  112.6 85.1 reduce-scatter.4
